TPU v7x, 32 devices: a whole 2x2x4 slice. The times are simulated.
32 devices in a mesh: strike: 8 (over z, y), depth: 4 (over x, core).
Axes of the slice: x: 2, y: 2, z: 4, core: 2. Of those that a mesh axis runs over, the one named last changes fastest.
Arguments:
- velocity: float32 [3, 128, 64, 256], P(None, 'strike', 'depth'), may hold values from -6 to 6
- stress: float32 [6, 128, 64, 256], P(None, 'strike', 'depth'), may hold values from -6 to 6
- material: int32 [128, 64, 256], P('strike', 'depth'), may hold values from 0 to 3
- patch_order: int32 [48], replicated, may hold values from 0 to 47, each once
- fault_params: float32 [4, 64, 48], P(None, 'depth', 'strike'), may hold values from -5 to 5, as said below
Outputs:
- velocity_out: float32 [3, 128, 64, 256], P(None, 'strike', 'depth')
- slip_rate: float32 [64, 48], P('depth', 'strike')
Inputs may be any that keep to these rules, and one draw needn't show every extreme that they name: `fault_params`: row 0 in 0.3 to 1.2, row 1 in -0.5 to 1.5, row 2 in 1 to 3, row 3 in -5 to 5. `patch_order`: each fault column exactly once.
All inputs are finite; a program needn't handle non-finite values.
Results may differ from a plain program's by a relative error of at most 0.0003.
Values sent between devices are 32-bit elements; how exact they have to be, the bound alone decides.
A program may use at most 64 MiB of HBM per device.

v0:
```python
import jax
import jax.numpy as jnp
from jax import lax
from jax.sharding import PartitionSpec as P

NEWTON = 8
BUOY = (1.0, 0.8, 0.6, 1.25)
C_ONE = 9.0 / 8.0
C_TWO = -1.0 / 24.0


def with_halo(value, sides, width):
    for axis, dim in sides:
        size, length = (lax.axis_size(axis), value.shape[dim])
        up = [(i, (i + 1) % size) for i in range(size - 1)]
        down = [(j, i) for i, j in up]
        last = lax.slice_in_dim(value, length - width, length, axis=dim)
        first = lax.slice_in_dim(value, 0, width, axis=dim)
        before = lax.ppermute(last, axis, up)
        after = lax.ppermute(first, axis, down)
        value = jnp.concatenate([before, value, after], axis=dim)
    return value


def inverse_sinh(value):
    magnitude = jnp.log(jnp.abs(value) + jnp.sqrt(1.0 + value * value))
    return jnp.where(value < 0, -magnitude, magnitude)


def minus_padded(padded, axis):
    width = padded.shape[axis] - 4

    def part(offset):
        return lax.slice_in_dim(padded, 2 + offset, 2 + offset + width, axis=axis)

    return C_ONE * (part(0) - part(-1)) + C_TWO * (part(1) - part(-2))


def plus_padded(padded, axis):
    width = padded.shape[axis] - 4

    def part(offset):
        return lax.slice_in_dim(padded, 2 + offset, 2 + offset + width, axis=axis)

    return C_ONE * (part(1) - part(0)) + C_TWO * (part(2) - part(-1))


def pad_normal(field):
    return jnp.pad(field, ((0, 0), (0, 0), (2, 2)))


def friction(tau_trial, params):
    coef, psi, normal_stress, background = (params[0], params[1], params[2], params[3])
    tau_total = tau_trial + background
    half_q = 0.5 * jnp.exp(psi / coef)
    scale = normal_stress * coef
    rate = jnp.zeros_like(tau_total)
    for step in range(NEWTON):
        arg_val = rate * half_q
        resid = tau_total - rate - scale * inverse_sinh(arg_val)
        slope = -1.0 - scale * half_q / jnp.sqrt(1.0 + arg_val * arg_val)
        rate = rate - 0.35 * resid / slope
    return rate


def per_device(velocity, stress, material, patch_order, fault_params):
    cx, cz, ny = (stress.shape[1], stress.shape[2], stress.shape[3])
    row = ny // 2
    stacked = jnp.stack([stress[0], stress[2], stress[3], stress[4], stress[5]])
    padded = with_halo(stacked, (("strike", 1), ("depth", 2)), 2)
    x_part = padded[:, :, 2:-2]
    z_part = padded[:, 2:-2, :]
    x_sxx, x_sxy, x_sxz = (x_part[0], x_part[2], x_part[3])
    z_sxz, z_syz, z_szz = (z_part[3], z_part[4], z_part[1])
    buoyancy = jnp.zeros(material.shape, jnp.float32)
    for index in range(4):
        buoyancy = buoyancy + (material == index).astype(jnp.float32) * BUOY[index]
    dxx = minus_padded(x_sxx, 0)
    vx = velocity[0] + 0.25 * buoyancy * (
        dxx + minus_padded(pad_normal(stress[3]), 2) + minus_padded(z_sxz, 1)
    )
    vy = velocity[1] + 0.25 * buoyancy * (
        plus_padded(x_sxy, 0) + plus_padded(pad_normal(stress[1]), 2) + minus_padded(z_syz, 1)
    )
    vz = velocity[2] + 0.25 * buoyancy * (
        plus_padded(x_sxz, 0) + plus_padded(pad_normal(stress[5]), 2) + plus_padded(z_szz, 1)
    )
    fault_cols = patch_order.shape[0]
    n_strike = lax.axis_size("strike")
    strike_pos = lax.axis_index("strike")
    first_tile = n_strike // 4
    fault_tiles = fault_cols // cx
    inside = jnp.logical_and(strike_pos >= first_tile, strike_pos < first_tile + fault_tiles)
    offset = jnp.clip(strike_pos - first_tile, 0, fault_tiles - 1) * cx
    selector = (patch_order[:, None] == jnp.arange(fault_cols, dtype=jnp.int32)[None, :]).astype(
        jnp.float32
    )
    local_traction = (stress[3, :, :, row] + 0.5 * dxx[:, :, row]).T
    blank = jnp.zeros((cz, fault_cols), jnp.float32)
    masked = jnp.where(inside, local_traction, 0.0)
    owned = lax.psum_scatter(
        jnp.dot(
            lax.dynamic_update_slice(blank, masked, (jnp.int32(0), offset)),
            selector.T,
            precision=lax.Precision.HIGHEST,
            preferred_element_type=jnp.float32,
        ),
        "strike",
        scatter_dimension=1,
        tiled=True,
    )
    slip_own = friction(owned, fault_params)
    slip_all = lax.all_gather(slip_own, "strike", axis=1, tiled=True)
    slip_tile = lax.dynamic_slice(
        jnp.dot(
            slip_all, selector, precision=lax.Precision.HIGHEST, preferred_element_type=jnp.float32
        ),
        (jnp.int32(0), offset),
        (cz, cx),
    )
    slip_planar = slip_tile.T
    plus_side = vx[:, :, row]
    minus_side = vx[:, :, row - 1]
    middle = 0.5 * (plus_side + minus_side)
    vx = vx.at[:, :, row].set(jnp.where(inside, middle + 0.5 * slip_planar, plus_side))
    vx = vx.at[:, :, row - 1].set(jnp.where(inside, middle - 0.5 * slip_planar, minus_side))
    return (jnp.stack([vx, vy, vz]), slip_own)


def solution(mesh):
    return jax.shard_map(
        per_device,
        mesh=mesh,
        in_specs=(
            P(None, "strike", "depth", None),
            P(None, "strike", "depth", None),
            P("strike", "depth", None),
            P(),
            P(None, "depth", "strike"),
        ),
        out_specs=(P(None, "strike", "depth", None), P("depth", "strike")),
        check_vma=False,
    )
```

profile of v0, /device:TPU:2, one launch (start us, length us, event | category | flops | bytes accessed | tf_op | source)
XLA Modules:
  0.0 105.1 jit_solution(18227903959645477159)
XLA Ops:
  0.6 0.0 copy-start
  0.6 2.1 %slice_bitcast_fusion.2 = (f32[16,16,256]{2,1,0:T(8,128)}, f32[16,16,256]{2,1,0:T(8,128)S(1)}, f32[1,16,16,256]{3,2,1,0:T(8,128)S(1)}, f32[16,16,256]{2,1,0:T(8,128)S(1)}) fusion(f32[6,16,16,256]{3,2,1,0:T(8,128)} %param.10), kind=kLoop, calls=%fused_computation.87 | loop fusion | bytes 2097152 | tf_op jit(solution)/shard_map/squeeze | solution.py:80
  2.7 0.0 copy-done
  2.7 0.0 copy-start.6
  2.7 0.1 slice.262
  2.8 0.0 copy-start.4
  2.8 1.3 %collective-permute-start.1 = (f32[5,2,16,256]{3,2,1,0:T(8,128)S(1)}, f32[5,2,16,256]{3,2,1,0:T(8,128)S(1)}, u32[]{:S(2)}, u32[]{:S(2)}) collective-permute-start(f32[5,2,16,256]{3,2,1,0:T(8,128)S(1)} %get-tuple-element.42), channel_id=1, source_target_pairs={{4,0},{8,4},{12,8},{16,12},{20,16},{24,20},{28,24},{5,1},{9,5},{13... | collective-permute-start | bytes 491528 | tf_op jit(solution)/shard_map/ppermute | solution.py:20
  4.1 4.6 %collective-permute-start = (f32[5,2,16,256]{3,2,1,0:T(8,128)S(1)}, f32[5,2,16,256]{3,2,1,0:T(8,128)S(1)}, u32[]{:S(2)}, u32[]{:S(2)}) collective-permute-start(f32[5,2,16,256]{3,2,1,0:T(8,128)S(1)} %get-tuple-element.41), channel_id=1, source_target_pairs={{0,4},{4,8},{8,12},{12,16},{16,20},{20,24},{24,28},{1,5},{5,9},{9,... | collective-permute-start | bytes 491528 | tf_op jit(solution)/shard_map/ppermute | solution.py:19
  8.7 0.2 copy.200
  8.9 0.0 copy-done.6
  8.9 0.6 dynamic-slice.16
  10.1 0.5 collective-permute-done.1
  10.7 3.4 %collective-permute-done = f32[5,2,16,256]{3,2,1,0:T(8,128)S(1)} collective-permute-done((f32[5,2,16,256]{3,2,1,0:T(8,128)S(1)}, f32[5,2,16,256]{3,2,1,0:T(8,128)S(1)}, u32[]{:S(2)}, u32[]{:S(2)}) %collective-permute-start) | collective-permute-done | bytes 163872 | tf_op jit(solution)/shard_map/ppermute | solution.py:19
  14.1 0.1 pad_maximum_fusion.13
  14.3 2.1 %collective-permute-start.3 = (f32[5,20,2,256]{3,2,1,0:T(2,128)S(1)}, f32[5,20,2,256]{3,2,1,0:T(2,128)S(1)}, u32[]{:S(2)}, u32[]{:S(2)}) collective-permute-start(f32[5,20,2,256]{3,2,1,0:T(2,128)S(1)} %get-tuple-element.36), channel_id=1, source_target_pairs={{1,0},{2,1},{3,2},{5,4},{6,5},{7,6},{9,8},{10,9},{11,10},{13,12},{... | collective-permute-start | bytes 614408 | tf_op jit(solution)/shard_map/ppermute | solution.py:20
  16.3 2.3 %collective-permute-start.2 = (f32[5,20,2,256]{3,2,1,0:T(2,128)S(1)}, f32[5,20,2,256]{3,2,1,0:T(2,128)S(1)}, u32[]{:S(2)}, u32[]{:S(2)}) collective-permute-start(f32[5,20,2,256]{3,2,1,0:T(2,128)S(1)} %get-tuple-element.35), channel_id=1, source_target_pairs={{0,1},{1,2},{2,3},{4,5},{5,6},{6,7},{8,9},{9,10},{10,11},{12,13},{... | collective-permute-start | bytes 614408 | tf_op jit(solution)/shard_map/ppermute | solution.py:19
  18.6 0.0 copy-done.4
  18.6 0.0 copy-start.1
  18.7 0.0 copy-start.2
  18.7 0.9 collective-permute-done.3
  19.6 3.8 %collective-permute-done.2 = f32[5,20,2,256]{3,2,1,0:T(2,128)S(1)} collective-permute-done((f32[5,20,2,256]{3,2,1,0:T(2,128)S(1)}, f32[5,20,2,256]{3,2,1,0:T(2,128)S(1)}, u32[]{:S(2)}, u32[]{:S(2)}) %collective-permute-start.2) | collective-permute-done | bytes 204832 | tf_op jit(solution)/shard_map/ppermute | solution.py:19
  23.4 0.2 maximum_bitcast_fusion.1
  23.6 0.0 copy-done.1
  23.6 0.0 copy-done.2
  23.6 0.0 copy-start.5
  23.6 1.3 %fusion.7 = (f32[16,16,256]{2,1,0:T(8,128)S(1)}, f32[16,16,256]{2,1,0:T(8,128)S(1)}) fusion(f32[16,16,256]{2,1,0:T(8,128)S(1)} %copy-done.2, f32[16,20,256]{2,1,0:T(8,128)S(1)} %get-tuple-element.32, f32[3,16,16,256]{3,2,1,0:T(8,128)} %param.9, s32[16,16,256]{2,1,0:T(8,128)S(1)} %copy-done.1, f32[4,16,16,256]{3,2,1,0:T(8,128)S(1)} %slice.262, ...), kind=kLoop, calls=%fused_computation.24 | loop fusion | flops 2424832 | bytes 3997696 | tf_op jit(solution)/shard_map/add | solution.py:79
  25.0 0.8 fusion.108
  25.7 1.1 %copy.199 = f32[16,16,1]{0,1,2:T(8,128)S(1)} copy(f32[16,16,1]{2,1,0:T(8,128)} %get-tuple-element.43) | data formatting | bytes 2048 | tf_op jit(solution)/shard_map/squeeze | solution.py:123
  26.8 1.1 %copy.193 = f32[16,16,1]{0,1,2:T(8,128)S(1)} copy(f32[16,16,1]{2,1,0:T(8,128)} %get-tuple-element.51) | data formatting | bytes 2048 | tf_op jit(solution)/shard_map/mul | solution.py:98
  27.9 0.2 dynamic_update_slice.3
  28.1 0.0 copy-done.5
  28.1 0.2 fusion.54
  28.3 36.0 %all-reduce.3 = f32[16,48]{0,1:T(8,128)S(1)} all-reduce(f32[16,48]{0,1:T(8,128)S(1)} %fusion.54), channel_id=2, replica_groups=mesh['strike'=8,'depth'=4] {'strike'}, use_global_device_ids=true, to_apply=%region_0.1.clone | all-reduce | flops 768 | bytes 6144
  64.3 0.2 fusion.103
  64.6 0.0 copy-start.3
  64.6 30.6 %all-gather = f32[8,6,16]{2,1,0:T(8,128)S(1)} all-gather(f32[1,6,16]{2,1,0:T(8,128)S(1)} %bitcast.174), channel_id=1, replica_groups=mesh['strike'=8,'depth'=4] {'strike'}, dimensions={0}, use_global_device_ids=true | all-gather | bytes 3456 | tf_op jit(solution)/shard_map/all_gather | solution.py:113
  95.2 0.2 fusion.53
  95.4 1.1 %copy.198 = f32[16,16,1]{0,1,2:T(8,128)S(1)} copy(f32[16,16,1]{2,1,0:T(8,128)} %get-tuple-element.44) | data formatting | bytes 2048 | tf_op jit(solution)/shard_map/squeeze | solution.py:122
  96.5 0.1 fusion.58
  96.6 0.8 copy.189
  97.4 0.8 copy.192
  98.2 1.0 scatter.6
  99.2 2.1 %scatter.9 = f32[1,16,16,256]{3,2,1,0:T(8,128)S(1)} dynamic-update-slice(f32[1,16,16,256]{3,2,1,0:T(8,128)S(1)} %scatter.6, f32[1,16,16,1]{3,2,1,0:T(8,128)} %copy.192, s32[]{:T(128)} %constant.89.clone.1, s32[]{:T(128)} %constant.89.clone.1, s32[]{:T(128)} %constant.89.clone.1, s32[]{:T(128)} %constant.111.clone.1) | dynamic-update-slice | bytes 2052 | tf_op jit(solution)/shard_map/scatter | solution.py:126
  101.4 1.4 %fusion.27 = f32[1,16,16,256]{3,2,1,0:T(8,128)S(1)} fusion(f32[16,16,256]{2,1,0:T(8,128)S(1)} %get-tuple-element.40, f32[16,20,256]{2,1,0:T(8,128)S(1)} %get-tuple-element.34, f32[5,2,16,256]{3,2,1,0:T(8,128)S(1)} %collective-permute-done, f32[4,16,16,256]{3,2,1,0:T(8,128)S(1)} %slice.262, f32[1,16,16,256]{3,2,1,0:T(8,128)S(1)} %get-tuple-element.39, ...), kind=kLoop, calls=%fused_computation.44 | loop fusion | flops 2424832 | bytes 3997696 | tf_op jit(solution)/shard_map/stack | solution.py:127
  102.8 0.0 copy-done.3
  102.8 1.4 %fusion.17 = f32[1,16,16,256]{3,2,1,0:T(8,128)S(1)} fusion(f32[16,16,256]{2,1,0:T(8,128)S(1)} %get-tuple-element.38, f32[16,20,256]{2,1,0:T(8,128)S(1)} %get-tuple-element.33, f32[5,2,16,256]{3,2,1,0:T(8,128)S(1)} %collective-permute-done, f32[4,16,16,256]{3,2,1,0:T(8,128)S(1)} %slice.262, f32[1,16,16,256]{3,2,1,0:T(8,128)S(1)} %get-tuple-element.39, ...), kind=kLoop, calls=%fused_computation.34 | loop fusion | flops 2424832 | bytes 3997696 | tf_op jit(solution)/shard_map/stack | solution.py:127
  104.2 0.9 pad_maximum_fusion
  (6 shorter events, 0.1 us)
Async XLA Ops:
  0.6 2.1 %copy-start = (f32[6,16,16,256]{3,2,1,0:T(8,128)S(1)}, f32[6,16,16,256]{3,2,1,0:T(8,128)}, u32[]{:S(2)}) copy-start(f32[6,16,16,256]{3,2,1,0:T(8,128)} %param.10) | copy-start | bytes 4718596
  2.7 6.2 %copy-start.6 = (u32[32]{0:T(128)S(1)}, u32[32]{0:T(128)}, u32[]{:S(2)}) copy-start(u32[32]{0:T(128)} %constant.121) | copy-start | bytes 388
  2.8 15.8 %copy-start.4 = (f32[4,16,6]{1,0,2:T(4,128)S(1)}, f32[4,16,6]{1,0,2:T(4,128)}, u32[]{:S(2)}) copy-start(f32[4,16,6]{1,0,2:T(4,128)} %param.13) | copy-start | bytes 4612
  2.8 7.8 %collective-permute-start.1 = (f32[5,2,16,256]{3,2,1,0:T(8,128)S(1)}, f32[5,2,16,256]{3,2,1,0:T(8,128)S(1)}, u32[]{:S(2)}, u32[]{:S(2)}) collective-permute-start(f32[5,2,16,256]{3,2,1,0:T(8,128)S(1)} %get-tuple-element.42), channel_id=1, source_target_pairs={{4,0},{8,4},{12,8},{16,12},{20,16},{24,20},{28,24},{5,1},{9,5},{13... | collective-permute-start | bytes 491528 | tf_op jit(solution)/shard_map/ppermute | solution.py:20
  4.1 10.0 %collective-permute-start = (f32[5,2,16,256]{3,2,1,0:T(8,128)S(1)}, f32[5,2,16,256]{3,2,1,0:T(8,128)S(1)}, u32[]{:S(2)}, u32[]{:S(2)}) collective-permute-start(f32[5,2,16,256]{3,2,1,0:T(8,128)S(1)} %get-tuple-element.41), channel_id=1, source_target_pairs={{0,4},{4,8},{8,12},{12,16},{16,20},{20,24},{24,28},{1,5},{5,9},{9,... | collective-permute-start | bytes 491528 | tf_op jit(solution)/shard_map/ppermute | solution.py:19
  14.3 5.3 %collective-permute-start.3 = (f32[5,20,2,256]{3,2,1,0:T(2,128)S(1)}, f32[5,20,2,256]{3,2,1,0:T(2,128)S(1)}, u32[]{:S(2)}, u32[]{:S(2)}) collective-permute-start(f32[5,20,2,256]{3,2,1,0:T(2,128)S(1)} %get-tuple-element.36), channel_id=1, source_target_pairs={{1,0},{2,1},{3,2},{5,4},{6,5},{7,6},{9,8},{10,9},{11,10},{13,12},{... | collective-permute-start | bytes 614408 | tf_op jit(solution)/shard_map/ppermute | solution.py:20
  16.3 7.1 %collective-permute-start.2 = (f32[5,20,2,256]{3,2,1,0:T(2,128)S(1)}, f32[5,20,2,256]{3,2,1,0:T(2,128)S(1)}, u32[]{:S(2)}, u32[]{:S(2)}) collective-permute-start(f32[5,20,2,256]{3,2,1,0:T(2,128)S(1)} %get-tuple-element.35), channel_id=1, source_target_pairs={{0,1},{1,2},{2,3},{4,5},{5,6},{6,7},{8,9},{9,10},{10,11},{12,13},{... | collective-permute-start | bytes 614408 | tf_op jit(solution)/shard_map/ppermute | solution.py:19
  18.6 5.0 %copy-start.1 = (s32[16,16,256]{2,1,0:T(8,128)S(1)}, s32[16,16,256]{2,1,0:T(8,128)}, u32[]{:S(2)}) copy-start(s32[16,16,256]{2,1,0:T(8,128)} %param.11) | copy-start | bytes 786436
  18.7 5.0 %copy-start.2 = (f32[16,16,256]{2,1,0:T(8,128)S(1)}, f32[16,16,256]{2,1,0:T(8,128)}, u32[]{:S(2)}) copy-start(f32[16,16,256]{2,1,0:T(8,128)} %get-tuple-element.37) | copy-start | bytes 786436
  23.6 4.5 %copy-start.5 = (s32[48]{0:T(128)S(1)}, s32[48]{0:T(128)}, u32[]{:S(2)}) copy-start(s32[48]{0:T(128)} %param.12) | copy-start | bytes 580
  64.6 38.2 %copy-start.3 = (f32[16,6]{0,1:T(8,128)}, f32[16,6]{0,1:T(8,128)S(1)}, u32[]{:S(2)}) copy-start(f32[16,6]{0,1:T(8,128)S(1)} %fusion.103) | copy-start | bytes 1156
where the time goes:
time: 106 us; the launch traced here: 105 us
  blocking collectives  66.6 us (63%)
  local copies, waits for them, and re-layouts  11.2 us (11%)
  starting transfers between devices  10.2 us (10%)
  waiting for transfers between devices  8.72 us (8%)
  other arithmetic  6.48 us (6%)
  between operations  1.5 us (1%)
    unnamed x1, blocking collectives  36 us
    all_gather x1, blocking collectives, per_device(): slip_all = lax.all_gather(slip_own, 'strike', axis=1, tiled=True)  30.6 us
    ppermute x2, waiting for transfers between devices, with_halo(): before = lax.ppermute(last, axis, up)  7.27 us
    ppermute x2, starting transfers between devices, with_halo(): before = lax.ppermute(last, axis, up)  6.83 us
    another operation x4, other arithmetic, per_device(): return (jnp.stack([vx, vy, vz]), slip_own)  3.81 us
    ppermute x2, starting transfers between devices, with_halo(): after = lax.ppermute(first, axis, down)  3.36 us
    scatter x1, local copies, waits for them, and re-layouts, per_device(): vx.at[:, :, row - 1]  2.14 us
  transfers between devices with their start and end apart: 4, of which 4 were waited for; matrix products, arithmetic and copies ran while one was open for 1% of the time, Pallas kernels for 0%

commit v1 on v0

--- a/solution.py
+++ b/solution.py
@@ -1,3 +1,4 @@
+import functools
 import jax
 import jax.numpy as jnp
 from jax import lax
@@ -7,6 +8,23 @@
 BUOY = (1.0, 0.8, 0.6, 1.25)
 C_ONE = 9.0 / 8.0
 C_TWO = -1.0 / 24.0
+
+
+def _order_scales(z, lane_axis):
+    n = jax.lax.axis_size(lane_axis)
+    seen = tuple(((b, (b + 1) % n) for b in range(n)))
+    pile = tuple(((b, (b - 1) % n) for b in range(n)))
+    long_array, block_now = ([z], [z])
+    for _ in range(n // 2):
+        long_array.append(jax.lax.ppermute(long_array[-1], axis_name=lane_axis, perm=seen))
+    for _ in range((n - 1) // 2):
+        local_out = jax.lax.ppermute(block_now[-1], axis_name=lane_axis, perm=pile)
+        block_now.append(local_out)
+    work_now = jnp.concatenate([*long_array[::-1], *block_now[1:]], axis=1)
+    return jnp.roll(work_now, shift=(jax.lax.axis_index(lane_axis) - n // 2) * z.shape[1], axis=1)
+
+
+name_the_tiles = functools.partial(_order_scales, lane_axis="strike")
 
 
 def with_halo(value, sides, width):
@@ -110,7 +128,7 @@
         tiled=True,
     )
     slip_own = friction(owned, fault_params)
-    slip_all = lax.all_gather(slip_own, "strike", axis=1, tiled=True)
+    slip_all = name_the_tiles(slip_own)
     slip_tile = lax.dynamic_slice(
         jnp.dot(
             slip_all, selector, precision=lax.Precision.HIGHEST, preferred_element_type=jnp.float32

time: 106 us -> 92 us (0.87)
  blocking collectives: 66.6 us -> 36 us
  starting transfers between devices: 10.2 us -> 24.6 us
  waiting for transfers between devices: 8.72 us -> 14.7 us
  local copies, waits for them, and re-layouts: 11.2 us -> 7.15 us
    all_gather x1 -> x0, blocking collectives: 30.6 us -> none  [per_device(): slip_all = lax.all_gather(slip_own, 'strike', axis=1, tiled=True)]
    ppermute x0 -> x7, starting transfers between devices: none -> 14.4 us  [the longest x3 14.3 us: _order_scales(): local_out = jax.lax.ppermute(block_now[-1], axis_name=lane_axis, perm=pile)]
    ppermute x0 -> x7, waiting for transfers between devices: none -> 6 us  [the longest x4 5.19 us: _order_scales(): jax.lax.ppermute(long_array[-1], axis_name=lane_axis, perm=seen)]
    another operation x2, local copies, waits for them, and re-layouts: 1.65 us -> 0.36 us  [per_device(): return (jnp.stack([vx, vy, vz]), slip_own)]
  transfers between devices with their start and end apart: 4 -> 11, of which waited for: 4 -> 8; matrix products, arithmetic and copies ran while one was open for 1% -> 7% of each run, Pallas kernels for 0% -> 0%
where the time goes in v1:
time: 92 us; the launch traced here: 91.6 us
  blocking collectives  36 us (39%)
  starting transfers between devices  24.6 us (27%)
  waiting for transfers between devices  14.7 us (16%)
  local copies, waits for them, and re-layouts  7.15 us (8%)
  other arithmetic  7.14 us (8%)
  between operations  1.57 us (2%)
    unnamed x1, blocking collectives  36 us
    ppermute x3, starting transfers between devices, _order_scales(): local_out = jax.lax.ppermute(block_now[-1], axis_name=lane_axis, perm=pile)  14.3 us
    ppermute x2, waiting for transfers between devices, with_halo(): before = lax.ppermute(last, axis, up)  7.27 us
    ppermute x2, starting transfers between devices, with_halo(): before = lax.ppermute(last, axis, up)  6.83 us
    ppermute x4, waiting for transfers between devices, _order_scales(): jax.lax.ppermute(long_array[-1], axis_name=lane_axis, perm=seen)  5.19 us
    another operation x4, other arithmetic, per_device(): return (jnp.stack([vx, vy, vz]), slip_own)  4.48 us
    ppermute x2, starting transfers between devices, with_halo(): after = lax.ppermute(first, axis, down)  3.36 us
    squeeze x1, local copies, waits for them, and re-layouts, per_device(): stress[3]  2.08 us
  transfers between devices with their start and end apart: 11, of which 8 were waited for; matrix products, arithmetic and copies ran while one was open for 7% of the time, Pallas kernels for 0%

profile of v1, /device:TPU:2, one launch (start us, length us, event | category | flops | bytes accessed | tf_op | source)
XLA Modules:
  0.0 91.6 jit_solution(6060813623670643838)
XLA Ops:
  0.6 0.0 copy-start
  0.6 2.1 %slice_bitcast_fusion.2 = (f32[16,16,256]{2,1,0:T(8,128)S(1)}, f32[16,16,256]{2,1,0:T(8,128)S(1)}, f32[1,16,16,256]{3,2,1,0:T(8,128)S(1)}, f32[16,16,256]{2,1,0:T(8,128)}) fusion(f32[6,16,16,256]{3,2,1,0:T(8,128)} %param.10), kind=kLoop, calls=%fused_computation.87 | loop fusion | bytes 2097152 | tf_op jit(solution)/shard_map/squeeze | solution.py:98
  2.7 0.0 copy-done
  2.7 0.1 slice.262
  2.8 0.0 copy-start.6
  2.8 0.0 copy-start.4
  2.8 1.3 %collective-permute-start.1 = (f32[5,2,16,256]{3,2,1,0:T(8,128)S(1)}, f32[5,2,16,256]{3,2,1,0:T(8,128)S(1)}, u32[]{:S(2)}, u32[]{:S(2)}) collective-permute-start(f32[5,2,16,256]{3,2,1,0:T(8,128)S(1)} %get-tuple-element.40), channel_id=1, source_target_pairs={{4,0},{8,4},{12,8},{16,12},{20,16},{24,20},{28,24},{5,1},{9,5},{13... | collective-permute-start | bytes 491528 | tf_op jit(solution)/shard_map/ppermute | solution.py:38
  4.1 4.6 %collective-permute-start = (f32[5,2,16,256]{3,2,1,0:T(8,128)S(1)}, f32[5,2,16,256]{3,2,1,0:T(8,128)S(1)}, u32[]{:S(2)}, u32[]{:S(2)}) collective-permute-start(f32[5,2,16,256]{3,2,1,0:T(8,128)S(1)} %get-tuple-element.39), channel_id=1, source_target_pairs={{0,4},{4,8},{8,12},{12,16},{16,20},{20,24},{24,28},{1,5},{5,9},{9,... | collective-permute-start | bytes 491528 | tf_op jit(solution)/shard_map/ppermute | solution.py:37
  8.8 0.2 copy.282
  8.9 0.6 dynamic-slice.16
  10.2 0.5 collective-permute-done.1
  10.7 3.4 %collective-permute-done = f32[5,2,16,256]{3,2,1,0:T(8,128)S(1)} collective-permute-done((f32[5,2,16,256]{3,2,1,0:T(8,128)S(1)}, f32[5,2,16,256]{3,2,1,0:T(8,128)S(1)}, u32[]{:S(2)}, u32[]{:S(2)}) %collective-permute-start) | collective-permute-done | bytes 163872 | tf_op jit(solution)/shard_map/ppermute | solution.py:37
  14.1 0.1 pad_maximum_fusion.13
  14.3 2.1 %collective-permute-start.3 = (f32[5,20,2,256]{3,2,1,0:T(2,128)S(1)}, f32[5,20,2,256]{3,2,1,0:T(2,128)S(1)}, u32[]{:S(2)}, u32[]{:S(2)}) collective-permute-start(f32[5,20,2,256]{3,2,1,0:T(2,128)S(1)} %get-tuple-element.34), channel_id=1, source_target_pairs={{1,0},{2,1},{3,2},{5,4},{6,5},{7,6},{9,8},{10,9},{11,10},{13,12},{... | collective-permute-start | bytes 614408 | tf_op jit(solution)/shard_map/ppermute | solution.py:38
  16.3 2.3 %collective-permute-start.2 = (f32[5,20,2,256]{3,2,1,0:T(2,128)S(1)}, f32[5,20,2,256]{3,2,1,0:T(2,128)S(1)}, u32[]{:S(2)}, u32[]{:S(2)}) collective-permute-start(f32[5,20,2,256]{3,2,1,0:T(2,128)S(1)} %get-tuple-element.33), channel_id=1, source_target_pairs={{0,1},{1,2},{2,3},{4,5},{5,6},{6,7},{8,9},{9,10},{10,11},{12,13},{... | collective-permute-start | bytes 614408 | tf_op jit(solution)/shard_map/ppermute | solution.py:37
  18.6 0.0 copy-done.4
  18.7 0.0 copy-start.1
  18.7 0.9 %collective-permute-done.3 = f32[5,20,2,256]{3,2,1,0:T(2,128)S(1)} collective-permute-done((f32[5,20,2,256]{3,2,1,0:T(2,128)S(1)}, f32[5,20,2,256]{3,2,1,0:T(2,128)S(1)}, u32[]{:S(2)}, u32[]{:S(2)}) %collective-permute-start.3) | collective-permute-done | bytes 204832 | tf_op jit(solution)/shard_map/ppermute | solution.py:38
  19.6 3.8 %collective-permute-done.2 = f32[5,20,2,256]{3,2,1,0:T(2,128)S(1)} collective-permute-done((f32[5,20,2,256]{3,2,1,0:T(2,128)S(1)}, f32[5,20,2,256]{3,2,1,0:T(2,128)S(1)}, u32[]{:S(2)}, u32[]{:S(2)}) %collective-permute-start.2) | collective-permute-done | bytes 204832 | tf_op jit(solution)/shard_map/ppermute | solution.py:37
  23.4 0.2 maximum_bitcast_fusion.1
  23.6 0.0 copy-done.1
  23.6 0.0 copy-start.5
  23.6 1.3 %fusion.7 = (f32[16,16,256]{2,1,0:T(8,128)S(1)}, f32[16,16,256]{2,1,0:T(8,128)S(1)}) fusion(f32[16,16,256]{2,1,0:T(8,128)S(1)} %get-tuple-element.35, f32[16,20,256]{2,1,0:T(8,128)S(1)} %get-tuple-element.30, f32[3,16,16,256]{3,2,1,0:T(8,128)} %param.9, s32[16,16,256]{2,1,0:T(8,128)S(1)} %copy-done.1, f32[4,16,16,256]{3,2,1,0:T(8,128)S(1)} %slice.262, ...), kind=kLoop, calls=%fused_computation.24 | loop fusion | flops 2424832 | bytes 3997696 | tf_op jit(solution)/shard_map/add | solution.py:97
  25.0 0.8 fusion.110
  25.7 0.2 copy.275
  25.9 0.2 dynamic_update_slice.3
  26.2 0.2 fusion.54
  26.4 36.0 %all-reduce.3 = f32[16,48]{0,1:T(8,128)S(1)} all-reduce(f32[16,48]{0,1:T(8,128)S(1)} %fusion.54), channel_id=2, replica_groups=mesh['strike'=8,'depth'=4] {'strike'}, use_global_device_ids=true, to_apply=%region_0.1.clone | all-reduce | flops 768 | bytes 6144
  62.4 0.2 fusion.104
  62.6 0.0 copy-start.3
  62.6 0.1 collective-permute-start.4
  62.7 4.7 %collective-permute-start.8 = (f32[16,6]{0,1:T(8,128)S(1)}, f32[16,6]{0,1:T(8,128)S(1)}, u32[]{:S(2)}, u32[]{:S(2)}) collective-permute-start(f32[16,6]{0,1:T(8,128)S(1)} %fusion.104), channel_id=1, source_target_pairs={{0,28},{4,0},{8,4},{12,8},{16,12},{20,16},{24,20},{28,24},{1,29},{... | collective-permute-start | bytes 1160 | tf_op jit(solution)/shard_map/ppermute | solution.py:21
  67.4 2.0 %fusion.27 = f32[1,16,16,256]{3,2,1,0:T(8,128)S(1)} fusion(f32[16,16,256]{2,1,0:T(8,128)} %get-tuple-element.38, f32[16,20,256]{2,1,0:T(8,128)S(1)} %get-tuple-element.32, f32[5,2,16,256]{3,2,1,0:T(8,128)S(1)} %collective-permute-done, f32[4,16,16,256]{3,2,1,0:T(8,128)S(1)} %slice.262, f32[1,16,16,256]{3,2,1,0:T(8,128)S(1)} %get-tuple-element.37, ...), kind=kLoop, calls=%fused_computation.44 | loop fusion | flops 2424832 | bytes 3997696 | tf_op jit(solution)/shard_map/stack | solution.py:145
  69.4 0.0 collective-permute-done.4
  69.4 0.1 collective-permute-start.5
  69.5 1.4 %fusion.17 = f32[1,16,16,256]{3,2,1,0:T(8,128)S(1)} fusion(f32[16,16,256]{2,1,0:T(8,128)S(1)} %get-tuple-element.36, f32[16,20,256]{2,1,0:T(8,128)S(1)} %get-tuple-element.31, f32[5,2,16,256]{3,2,1,0:T(8,128)S(1)} %collective-permute-done, f32[4,16,16,256]{3,2,1,0:T(8,128)S(1)} %slice.262, f32[1,16,16,256]{3,2,1,0:T(8,128)S(1)} %get-tuple-element.37, ...), kind=kLoop, calls=%fused_computation.34 | loop fusion | flops 2424832 | bytes 3997696 | tf_op jit(solution)/shard_map/stack | solution.py:145
  70.9 0.0 collective-permute-done.8
  70.9 4.7 %collective-permute-start.9 = (f32[16,6]{0,1:T(8,128)S(1)}, f32[16,6]{0,1:T(8,128)S(1)}, u32[]{:S(2)}, u32[]{:S(2)}) collective-permute-start(f32[16,6]{0,1:T(8,128)S(1)} %collective-permute-done.8), channel_id=1, source_target_pairs={{0,28},{4,0},{8,4},{12,8},{16,12},{20,16},{24,20},{28,24},{1,29},{... | collective-permute-start | bytes 1160 | tf_op jit(solution)/shard_map/ppermute | solution.py:21
  75.7 0.1 collective-permute-done.5
  75.8 0.0 collective-permute-start.6
  75.8 0.1 copy.256
  75.9 1.1 %copy.281 = f32[16,16,1]{0,1,2:T(8,128)S(1)} copy(f32[16,16,1]{2,1,0:T(8,128)} %get-tuple-element.41) | data formatting | bytes 2048 | tf_op jit(solution)/shard_map/squeeze | solution.py:141
  77.0 0.2 copy.280
  77.1 0.0 collective-permute-done.9
  77.1 4.9 %collective-permute-start.10 = (f32[16,6]{0,1:T(8,128)S(1)}, f32[16,6]{0,1:T(8,128)S(1)}, u32[]{:S(2)}, u32[]{:S(2)}) collective-permute-start(f32[16,6]{0,1:T(8,128)S(1)} %collective-permute-done.9), channel_id=1, source_target_pairs={{0,28},{4,0},{8,4},{12,8},{16,12},{20,16},{24,20},{28,24},{1,29},{... | collective-permute-start | bytes 1160 | tf_op jit(solution)/shard_map/ppermute | solution.py:21
  82.0 0.1 collective-permute-done.6
  82.1 0.0 collective-permute-start.7
  82.1 0.1 copy.255
  82.2 0.1 copy.257
  82.3 0.1 copy.254
  82.3 0.1 copy.258
  82.4 0.1 copy.253
  82.5 0.8 collective-permute-done.10
  83.3 0.1 copy.259
  83.4 5.0 %collective-permute-done.7 = f32[16,6]{0,1:T(8,128)S(1)} collective-permute-done((f32[16,6]{0,1:T(8,128)S(1)}, f32[16,6]{0,1:T(8,128)S(1)}, u32[]{:S(2)}, u32[]{:S(2)}) %collective-permute-start.7) | collective-permute-done | bytes 416 | tf_op jit(solution)/shard_map/ppermute | solution.py:19
  88.4 0.1 copy.252
  88.5 0.1 concatenate.33
  88.6 0.2 fusion.53
  88.8 0.1 fusion.58
  88.9 0.2 copy.271
  89.1 0.2 copy.274
  89.2 0.2 scatter.6
  89.4 1.2 %scatter.9 = f32[1,16,16,256]{3,2,1,0:T(8,128)S(1)} dynamic-update-slice(f32[1,16,16,256]{3,2,1,0:T(8,128)S(1)} %scatter.6, f32[1,16,16,1]{3,2,1,0:T(8,128)S(1)} %copy.274, s32[]{:T(128)} %constant.108.clone.1, s32[]{:T(128)} %constant.108.clone.1, s32[]{:T(128)} %constant.108.clone.1, s32[]{:T(128)} %constant.133.clone.1) | dynamic-update-slice | bytes 2052 | tf_op jit(solution)/shard_map/scatter | solution.py:144
  90.7 0.9 %pad_maximum_fusion = f32[3,16,16,256]{3,2,1,0:T(8,128)} fusion(f32[1,16,16,256]{3,2,1,0:T(8,128)S(1)} %fusion.27, f32[1,16,16,256]{3,2,1,0:T(8,128)S(1)} %fusion.17, f32[1,16,16,256]{3,2,1,0:T(8,128)S(1)} %scatter.9), kind=kLoop, calls=%fused_computation | loop fusion | flops 393216 | bytes 1572864 | tf_op jit(solution)/shard_map/stack | solution.py:145
  (10 shorter events, 0.1 us)
Async XLA Ops:
  0.6 2.1 %copy-start = (f32[6,16,16,256]{3,2,1,0:T(8,128)S(1)}, f32[6,16,16,256]{3,2,1,0:T(8,128)}, u32[]{:S(2)}) copy-start(f32[6,16,16,256]{3,2,1,0:T(8,128)} %param.10) | copy-start | bytes 4718596
  2.8 6.2 %copy-start.6 = (u32[32]{0:T(128)S(1)}, u32[32]{0:T(128)}, u32[]{:S(2)}) copy-start(u32[32]{0:T(128)} %constant.143) | copy-start | bytes 388
  2.8 15.8 %copy-start.4 = (f32[4,16,6]{1,0,2:T(4,128)S(1)}, f32[4,16,6]{1,0,2:T(4,128)}, u32[]{:S(2)}) copy-start(f32[4,16,6]{1,0,2:T(4,128)} %param.13) | copy-start | bytes 4612
  2.8 7.8 %collective-permute-start.1 = (f32[5,2,16,256]{3,2,1,0:T(8,128)S(1)}, f32[5,2,16,256]{3,2,1,0:T(8,128)S(1)}, u32[]{:S(2)}, u32[]{:S(2)}) collective-permute-start(f32[5,2,16,256]{3,2,1,0:T(8,128)S(1)} %get-tuple-element.40), channel_id=1, source_target_pairs={{4,0},{8,4},{12,8},{16,12},{20,16},{24,20},{28,24},{5,1},{9,5},{13... | collective-permute-start | bytes 491528 | tf_op jit(solution)/shard_map/ppermute | solution.py:38
  4.1 10.0 %collective-permute-start = (f32[5,2,16,256]{3,2,1,0:T(8,128)S(1)}, f32[5,2,16,256]{3,2,1,0:T(8,128)S(1)}, u32[]{:S(2)}, u32[]{:S(2)}) collective-permute-start(f32[5,2,16,256]{3,2,1,0:T(8,128)S(1)} %get-tuple-element.39), channel_id=1, source_target_pairs={{0,4},{4,8},{8,12},{12,16},{16,20},{20,24},{24,28},{1,5},{5,9},{9,... | collective-permute-start | bytes 491528 | tf_op jit(solution)/shard_map/ppermute | solution.py:37
  14.3 5.3 %collective-permute-start.3 = (f32[5,20,2,256]{3,2,1,0:T(2,128)S(1)}, f32[5,20,2,256]{3,2,1,0:T(2,128)S(1)}, u32[]{:S(2)}, u32[]{:S(2)}) collective-permute-start(f32[5,20,2,256]{3,2,1,0:T(2,128)S(1)} %get-tuple-element.34), channel_id=1, source_target_pairs={{1,0},{2,1},{3,2},{5,4},{6,5},{7,6},{9,8},{10,9},{11,10},{13,12},{... | collective-permute-start | bytes 614408 | tf_op jit(solution)/shard_map/ppermute | solution.py:38
  16.3 7.1 %collective-permute-start.2 = (f32[5,20,2,256]{3,2,1,0:T(2,128)S(1)}, f32[5,20,2,256]{3,2,1,0:T(2,128)S(1)}, u32[]{:S(2)}, u32[]{:S(2)}) collective-permute-start(f32[5,20,2,256]{3,2,1,0:T(2,128)S(1)} %get-tuple-element.33), channel_id=1, source_target_pairs={{0,1},{1,2},{2,3},{4,5},{5,6},{6,7},{8,9},{9,10},{10,11},{12,13},{... | collective-permute-start | bytes 614408 | tf_op jit(solution)/shard_map/ppermute | solution.py:37
  18.7 5.0 %copy-start.1 = (s32[16,16,256]{2,1,0:T(8,128)S(1)}, s32[16,16,256]{2,1,0:T(8,128)}, u32[]{:S(2)}) copy-start(s32[16,16,256]{2,1,0:T(8,128)} %param.11) | copy-start | bytes 786436
  23.6 2.5 %copy-start.5 = (s32[48]{0:T(128)S(1)}, s32[48]{0:T(128)}, u32[]{:S(2)}) copy-start(s32[48]{0:T(128)} %param.12) | copy-start | bytes 580
  62.6 13.2 %copy-start.3 = (f32[16,6]{0,1:T(8,128)}, f32[16,6]{0,1:T(8,128)S(1)}, u32[]{:S(2)}) copy-start(f32[16,6]{0,1:T(8,128)S(1)} %fusion.104) | copy-start | bytes 1156
  62.6 6.8 %collective-permute-start.4 = (f32[16,6]{0,1:T(8,128)S(1)}, f32[16,6]{0,1:T(8,128)S(1)}, u32[]{:S(2)}, u32[]{:S(2)}) collective-permute-start(f32[16,6]{0,1:T(8,128)S(1)} %fusion.104), channel_id=1, source_target_pairs={{0,4},{4,8},{8,12},{12,16},{16,20},{20,24},{24,28},{28,0},{1,5},{5... | collective-permute-start | bytes 1160 | tf_op jit(solution)/shard_map/ppermute | solution.py:19
  62.7 8.3 %collective-permute-start.8 = (f32[16,6]{0,1:T(8,128)S(1)}, f32[16,6]{0,1:T(8,128)S(1)}, u32[]{:S(2)}, u32[]{:S(2)}) collective-permute-start(f32[16,6]{0,1:T(8,128)S(1)} %fusion.104), channel_id=1, source_target_pairs={{0,28},{4,0},{8,4},{12,8},{16,12},{20,16},{24,20},{28,24},{1,29},{... | collective-permute-start | bytes 1160 | tf_op jit(solution)/shard_map/ppermute | solution.py:21
  69.4 6.4 %collective-permute-start.5 = (f32[16,6]{0,1:T(8,128)S(1)}, f32[16,6]{0,1:T(8,128)S(1)}, u32[]{:S(2)}, u32[]{:S(2)}) collective-permute-start(f32[16,6]{0,1:T(8,128)S(1)} %collective-permute-done.4), channel_id=1, source_target_pairs={{0,4},{4,8},{8,12},{12,16},{16,20},{20,24},{24,28},{28,0},{1,5},{5... | collective-permute-start | bytes 1160 | tf_op jit(solution)/shard_map/ppermute | solution.py:19
  69.5 7.5 %copy-start.2 = (f32[16,16,1]{2,1,0:T(8,128)S(1)}, f32[16,16,1]{2,1,0:T(8,128)}, u32[]{:S(2)}) copy-start(f32[16,16,1]{2,1,0:T(8,128)} %get-tuple-element.42) | copy-start | bytes 3076
  70.9 6.2 %collective-permute-start.9 = (f32[16,6]{0,1:T(8,128)S(1)}, f32[16,6]{0,1:T(8,128)S(1)}, u32[]{:S(2)}, u32[]{:S(2)}) collective-permute-start(f32[16,6]{0,1:T(8,128)S(1)} %collective-permute-done.8), channel_id=1, source_target_pairs={{0,28},{4,0},{8,4},{12,8},{16,12},{20,16},{24,20},{28,24},{1,29},{... | collective-permute-start | bytes 1160 | tf_op jit(solution)/shard_map/ppermute | solution.py:21
  75.8 6.3 %collective-permute-start.6 = (f32[16,6]{0,1:T(8,128)S(1)}, f32[16,6]{0,1:T(8,128)S(1)}, u32[]{:S(2)}, u32[]{:S(2)}) collective-permute-start(f32[16,6]{0,1:T(8,128)S(1)} %collective-permute-done.5), channel_id=1, source_target_pairs={{0,4},{4,8},{8,12},{12,16},{16,20},{20,24},{24,28},{28,0},{1,5},{5... | collective-permute-start | bytes 1160 | tf_op jit(solution)/shard_map/ppermute | solution.py:19
  77.1 6.2 %collective-permute-start.10 = (f32[16,6]{0,1:T(8,128)S(1)}, f32[16,6]{0,1:T(8,128)S(1)}, u32[]{:S(2)}, u32[]{:S(2)}) collective-permute-start(f32[16,6]{0,1:T(8,128)S(1)} %collective-permute-done.9), channel_id=1, source_target_pairs={{0,28},{4,0},{8,4},{12,8},{16,12},{20,16},{24,20},{28,24},{1,29},{... | collective-permute-start | bytes 1160 | tf_op jit(solution)/shard_map/ppermute | solution.py:21
  82.1 6.3 %collective-permute-start.7 = (f32[16,6]{0,1:T(8,128)S(1)}, f32[16,6]{0,1:T(8,128)S(1)}, u32[]{:S(2)}, u32[]{:S(2)}) collective-permute-start(f32[16,6]{0,1:T(8,128)S(1)} %collective-permute-done.6), channel_id=1, source_target_pairs={{0,4},{4,8},{8,12},{12,16},{16,20},{20,24},{24,28},{28,0},{1,5},{5... | collective-permute-start | bytes 1160 | tf_op jit(solution)/shard_map/ppermute | solution.py:19
